TPU v7x, 32 devices: a whole 2x2x4 slice. The times are simulated.
32 devices in a mesh: ctx: 4 (over y, x), exp: 8 (over z, core).
Axes of the slice: x: 2, y: 2, z: 4, core: 2. Of those that a mesh axis runs over, the one named last changes fastest.
Arguments:
- hidden_in: bfloat16 [1024, 2048], P(('ctx', 'exp')), may hold values from -6 to 6
- queries: bfloat16 [1024, 4096], P('ctx', 'exp'), may hold values from -200 to 200
- keyvals: bfloat16 [1024, 512], P('ctx'), may hold values from -6 to 6
- out_weight: bfloat16 [4096, 2048], P('exp'), may hold values from -0.09375 to 0.09375
- norm_gain: float32 [2048], replicated, may hold values from 0.5 to 1.5
- router_weight: bfloat16 [2048, 16], replicated, may hold values from -0.125 to 0.125
- expert_gate_up: bfloat16 [16, 2048, 1536], P('exp', 'ctx'), may hold values from -0.125 to 0.125
- expert_down: bfloat16 [16, 768, 2048], P('exp', 'ctx'), may hold values from -0.21875 to 0.21875
- route_ids: int32 [1024, 8], P(('ctx', 'exp')), may hold values from 0 to 15, all different within a row; in each aligned block of 32 rows (0 to 31, 32 to 63, ...) at most 18 rows name the same one
- upstream: bfloat16 [1024, 2048], P(('ctx', 'exp')), may hold values from -6 to 6
Outputs:
- layer_out: bfloat16 [1024, 2048], P(('ctx', 'exp'))
- input_grad: bfloat16 [1024, 2048], P(('ctx', 'exp'))
- query_grad: bfloat16 [1024, 4096], P('ctx', 'exp')
- out_weight_grad: float32 [4096, 2048], P('exp', 'ctx')
- gate_up_grad: float32 [16, 2048, 1536], P('exp', 'ctx')
- down_grad: float32 [16, 768, 2048], P('exp', 'ctx')
- router_grad: float32 [2048, 16], replicated
- gain_grad: float32 [2048], replicated
Inputs may be any that keep to these rules, and one draw needn't show every extreme that they name: `route_ids`: each row names 8 different experts. In each aligned block of 32 rows (the rows of one device) no expert is named by more than 18 rows, a bound that some block reaches.
All inputs are finite; a program needn't handle non-finite values.
Results may differ from a plain program's by a relative error of at most 0.02.
Values may be sent and summed in bfloat16 or wider, within the bound.
A program may use at most 128 MiB of HBM per device.

v0:
```python
import jax
import jax.numpy as jnp
from jax import lax
from jax.sharding import PartitionSpec as P

D = 2048
HEAD_WIDTH = 128
QUERY_HEADS = 32
KEY_VALUE_HEADS = 2
FFE = 768
EXPERTS = 16
CAP = 18


norm_eps = 1e-06


def from_behind(shard, axis, by):
    count = lax.axis_size(axis)
    pairs = [(i, i + by) for i in range(count) if 0 <= i + by < count]
    return lax.ppermute(shard, axis, pairs)


def per_device(
    hidden_in,
    queries,
    keyvals,
    out_weight,
    norm_gain,
    router_weight,
    expert_gate_up,
    expert_down,
    route_ids,
    upstream,
):
    ctx_count = lax.axis_size("ctx")
    ctx_index = lax.axis_index("ctx")
    expert_number = lax.axis_index("exp")
    tok_ctx = queries.shape[0]
    local_heads = queries.shape[1] // HEAD_WIDTH
    score_scale = HEAD_WIDTH ** (-0.5)
    keyvalue_head = expert_number * local_heads // (QUERY_HEADS // KEY_VALUE_HEADS)
    own_block = lax.dynamic_slice_in_dim(keyvals, keyvalue_head * 2 * HEAD_WIDTH, 2 * HEAD_WIDTH, 1)
    query_heads = queries.reshape(tok_ctx, local_heads, HEAD_WIDTH)
    query_pos = ctx_index * tok_ctx + jnp.arange(tok_ctx, dtype=jnp.int32)
    key_offsets = jnp.arange(tok_ctx, dtype=jnp.int32)

    def block_scores(kv_block, anchor):
        scores = (
            jnp.einsum(
                "qhd,kd->qhk",
                query_heads,
                kv_block[:, :HEAD_WIDTH],
                preferred_element_type=jnp.float32,
            )
            * score_scale
        )
        allowed = (anchor * tok_ctx + key_offsets)[None, :] <= query_pos[:, None]
        return jnp.where(allowed[:, None, :], scores, -jnp.inf)

    def absorb(running, kv_block, anchor):
        row_max, row_sum, mixed = running
        scores = block_scores(kv_block, anchor)
        new_max = jnp.maximum(row_max, jnp.max(scores, axis=2))
        weights = jnp.exp(scores - new_max[:, :, None])
        decay_factor = jnp.exp(row_max - new_max)
        row_sum = row_sum * decay_factor + jnp.sum(weights, axis=2)
        mixed = mixed * decay_factor[:, :, None] + jnp.einsum(
            "qhk,kd->qhd",
            weights.astype(jnp.bfloat16),
            kv_block[:, HEAD_WIDTH:],
            preferred_element_type=jnp.float32,
        )
        return (new_max, row_sum, mixed)

    start_running = (
        jnp.full((tok_ctx, local_heads), -jnp.inf, jnp.float32),
        jnp.zeros((tok_ctx, local_heads), jnp.float32),
        jnp.zeros((tok_ctx, local_heads, HEAD_WIDTH), jnp.float32),
    )
    running = absorb(start_running, own_block, ctx_index)
    stored = jnp.zeros((ctx_count, tok_ctx, 2 * HEAD_WIDTH), own_block.dtype)
    stored = lax.dynamic_update_index_in_dim(stored, own_block, ctx_index, 0)

    def forward_step(hop_count, loop_state):
        kv_block, running, stored = loop_state
        kv_block = from_behind(kv_block, "ctx", 1)
        anchor = ctx_index - hop_count

        def use_block():
            return (
                absorb(running, kv_block, anchor),
                lax.dynamic_update_index_in_dim(stored, kv_block, anchor, 0),
            )

        def skip_block():
            return (running, stored)

        running, stored = lax.cond(hop_count <= ctx_index, use_block, skip_block)
        return (kv_block, running, stored)

    final_block, running, stored = lax.fori_loop(
        1, ctx_count, forward_step, (own_block, running, stored)
    )
    row_max, row_sum, mixed = running
    attention = (mixed / row_sum[:, :, None]).astype(jnp.bfloat16)
    log_total = row_max + jnp.log(row_sum)
    attention_flat = attention.reshape(tok_ctx, local_heads * HEAD_WIDTH)
    rows_here = attention_flat
    projected = lax.psum_scatter(
        jnp.dot(rows_here, out_weight, preferred_element_type=jnp.float32).astype(jnp.bfloat16),
        "exp",
        scatter_dimension=0,
        tiled=True,
    ).astype(jnp.float32)
    residual = hidden_in.astype(jnp.float32) + projected
    inv_rms = lax.rsqrt(jnp.mean(residual * residual, axis=1, keepdims=True) + norm_eps)
    normed = (residual * inv_rms * norm_gain).astype(jnp.bfloat16)
    expert_hit = route_ids[:, :, None] == jnp.arange(EXPERTS, dtype=jnp.int32)
    hit_any = jnp.any(expert_hit, axis=1).astype(jnp.int32)
    earlier = jnp.cumsum(hit_any, axis=0) - hit_any
    slot_index = jnp.sum(jnp.where(expert_hit, earlier[:, None, :], 0), axis=2)
    flat_slot = route_ids * CAP + slot_index
    dispatch = (flat_slot[:, :, None] == jnp.arange(EXPERTS * CAP, dtype=jnp.int32)).astype(
        jnp.bfloat16
    )
    logits = jnp.dot(normed, router_weight, preferred_element_type=jnp.float32)
    chosen = jnp.sum(jnp.where(expert_hit, logits[:, None, :], 0.0), axis=2)
    route_probs = jax.nn.softmax(chosen, axis=1)
    outgoing = (
        jnp.einsum("tks,td->sd", dispatch, normed, preferred_element_type=jnp.float32)
        .astype(jnp.bfloat16)
        .reshape(EXPERTS, CAP, D)
    )
    arrived = lax.all_to_all(outgoing, "exp", split_axis=0, concat_axis=1, tiled=True)
    gate_up_full, down_full = (
        lax.all_gather(expert_gate_up, "ctx", axis=1, tiled=True),
        lax.all_gather(expert_down, "ctx", axis=1, tiled=True),
    )
    gate_up = jnp.einsum("erd,edf->erf", arrived, gate_up_full, preferred_element_type=jnp.float32)
    gate_part = gate_up[:, :, :FFE]
    up_part = gate_up[:, :, FFE:]
    activation = (jax.nn.silu(gate_part) * up_part).astype(jnp.bfloat16)
    expert_out = jnp.einsum(
        "erf,efd->erd", activation, down_full, preferred_element_type=jnp.float32
    ).astype(jnp.bfloat16)
    coming_back = lax.all_to_all(expert_out, "exp", split_axis=1, concat_axis=0, tiled=True)
    returned = jnp.einsum(
        "tks,sd->tkd",
        dispatch,
        coming_back.reshape(EXPERTS * CAP, D),
        preferred_element_type=jnp.float32,
    )
    mixture = jnp.sum(route_probs[:, :, None] * returned, axis=1)
    layer_out = (residual + mixture).astype(jnp.bfloat16)
    out_grad = upstream.astype(jnp.float32)
    row_grads = (route_probs[:, :, None] * out_grad[:, None, :]).astype(jnp.bfloat16)
    prob_grads = jnp.sum(returned * out_grad[:, None, :], axis=2)
    grad_outgoing = (
        jnp.einsum("tks,tkd->sd", dispatch, row_grads, preferred_element_type=jnp.float32)
        .astype(jnp.bfloat16)
        .reshape(EXPERTS, CAP, D)
    )
    grad_arrived = lax.all_to_all(grad_outgoing, "exp", split_axis=0, concat_axis=1, tiled=True)
    gate_up_back, down_back = (gate_up_full, down_full)
    act_grad = jnp.einsum(
        "erd,efd->erf", grad_arrived, down_back, preferred_element_type=jnp.float32
    )
    sigmoid_gate = jax.nn.sigmoid(gate_part)
    gate_grad = act_grad * up_part * sigmoid_gate * (1.0 + gate_part * (1.0 - sigmoid_gate))
    up_grad = act_grad * gate_part * sigmoid_gate
    pair_grad = jnp.concatenate([gate_grad, up_grad], axis=2).astype(jnp.bfloat16)
    down_term = jnp.einsum(
        "erf,erd->efd", activation, grad_arrived, preferred_element_type=jnp.float32
    )
    gate_up_term = jnp.einsum(
        "erd,erf->edf", arrived, pair_grad, preferred_element_type=jnp.float32
    )
    rows_back = jnp.einsum(
        "erf,edf->erd", pair_grad, gate_up_back, preferred_element_type=jnp.float32
    ).astype(jnp.bfloat16)
    grad_returned = lax.all_to_all(rows_back, "exp", split_axis=1, concat_axis=0, tiled=True)
    gate_up_grad, down_grad = (
        lax.psum_scatter(
            gate_up_term.astype(jnp.bfloat16), "ctx", scatter_dimension=1, tiled=True
        ).astype(jnp.float32),
        lax.psum_scatter(
            down_term.astype(jnp.bfloat16), "ctx", scatter_dimension=1, tiled=True
        ).astype(jnp.float32),
    )
    expert_part = jnp.einsum(
        "tks,sd->td",
        dispatch,
        grad_returned.reshape(EXPERTS * CAP, D),
        preferred_element_type=jnp.float32,
    )
    chosen_grad = route_probs * (
        prob_grads - jnp.sum(route_probs * prob_grads, axis=1, keepdims=True)
    )
    logit_grad = jnp.sum(jnp.where(expert_hit, chosen_grad[:, :, None], 0.0), axis=1)
    normed_float = normed.astype(jnp.float32)
    router_term = jnp.einsum("td,te->de", normed_float, logit_grad, precision=lax.Precision.HIGHEST)
    normed_grad = expert_part + jnp.einsum(
        "te,de->td", logit_grad, router_weight.astype(jnp.float32), precision=lax.Precision.HIGHEST
    )
    gain_term = jnp.sum(normed_grad * residual * inv_rms, axis=0)
    router_grad, gain_grad = lax.psum((router_term, gain_term), ("ctx", "exp"))
    inner_mean = jnp.mean(residual * norm_gain * normed_grad, axis=1, keepdims=True)
    input_grad = (
        out_grad + norm_gain * inv_rms * normed_grad - residual * inv_rms**3 * inner_mean
    ).astype(jnp.bfloat16)
    arriving = lax.all_gather(input_grad, "exp", axis=0, tiled=True)
    rows_here = attention_flat
    weight_part = jnp.einsum("tc,td->cd", rows_here, arriving, preferred_element_type=jnp.float32)
    new_rows = jnp.einsum("td,cd->tc", arriving, out_weight, preferred_element_type=jnp.float32)
    attn_part = new_rows
    weight_part, attn_part = (weight_part, attn_part)
    out_weight_grad = lax.psum_scatter(
        weight_part.astype(jnp.bfloat16), "ctx", scatter_dimension=1, tiled=True
    ).astype(jnp.float32)
    attention_grad = attn_part.astype(jnp.bfloat16).reshape(tok_ctx, local_heads, HEAD_WIDTH)
    delta_rows = jnp.sum(attention_grad.astype(jnp.float32) * attention.astype(jnp.float32), axis=2)

    def release(query_acc, kv_block, anchor):
        scores = block_scores(kv_block, anchor)
        attn_probs = jnp.exp(scores - log_total[:, :, None])
        prob_part = jnp.einsum(
            "qhd,kd->qhk",
            attention_grad,
            kv_block[:, HEAD_WIDTH:],
            preferred_element_type=jnp.float32,
        )
        score_grad = (attn_probs * (prob_part - delta_rows[:, :, None])).astype(jnp.bfloat16)
        return query_acc + jnp.einsum(
            "qhk,kd->qhd", score_grad, kv_block[:, :HEAD_WIDTH], preferred_element_type=jnp.float32
        )

    query_acc = release(
        jnp.zeros((tok_ctx, local_heads, HEAD_WIDTH), jnp.float32), own_block, ctx_index
    )

    def back_step(hop_count, query_sum):
        anchor = ctx_index - hop_count
        kv_block = lax.dynamic_index_in_dim(stored, jnp.maximum(anchor, 0), 0, keepdims=False)
        return lax.cond(
            hop_count <= ctx_index, lambda: release(query_sum, kv_block, anchor), lambda: query_sum
        )

    query_acc = lax.fori_loop(1, ctx_count, back_step, query_acc)
    query_grad = (
        (score_scale * query_acc).astype(jnp.bfloat16).reshape(tok_ctx, local_heads * HEAD_WIDTH)
    )
    return (
        layer_out,
        input_grad,
        query_grad,
        out_weight_grad,
        gate_up_grad,
        down_grad,
        router_grad,
        gain_grad,
    )


def solution(mesh):
    return jax.shard_map(
        per_device,
        mesh=mesh,
        in_specs=(
            P(("ctx", "exp"), None),
            P("ctx", "exp"),
            P("ctx", None),
            P("exp", None),
            P(),
            P(),
            P("exp", "ctx", None),
            P("exp", "ctx", None),
            P(("ctx", "exp"), None),
            P(("ctx", "exp"), None),
        ),
        out_specs=(
            P(("ctx", "exp"), None),
            P(("ctx", "exp"), None),
            P("ctx", "exp"),
            P("exp", "ctx"),
            P("exp", "ctx", None),
            P("exp", "ctx", None),
            P(),
            P(),
        ),
        check_vma=False,
    )
```

profile of v0, /device:TPU:0, one launch (start us, length us, event | category | flops | bytes accessed | tf_op | source)
XLA Modules:
  0.0 623.0 jit_solution(4528615251474178917)
XLA Ops:
  14.2 25.3 %while.39 = (s32[]{:T(128)}, bf16[256,256]{1,0:T(8,128)(2,1)}, f32[256,4]{0,1:T(4,128)S(1)}, f32[256,4]{0,1:T(4,128)S(1)}, f32[256,4,128]{2,0,1:T(8,128)S(1)}, /...) while((s32[]{:T(128)}, bf16[256,256]{1,0:T(8,128)(2,1)}, ...), condition=%wide.region_7.8_spmd.clone, body=%wide.region_2.7_spmd.clone.sunk | while | flops 136382976 | bytes 5840257 | solution.py:102
  14.3 4.9 collective-permute-start
  22.8 5.5 collective-permute-start
  31.8 4.3 collective-permute-start
  44.7 36.2 %reduce-scatter.5.cloned.1.call-done = bf16[32,2048]{1,0:T(8,128)(2,1)} async-done(((bf16[256,2048]{1,0:T(8,128)(2,1)}), bf16[32,2048]{1,0:T(8,128)(2,1)}) %reduce-scatter.5.cloned.1.call-update) | async-done | bytes 131088 | tf_op jit(solution)/shard_map/reduce_scatter | solution.py:110
  87.0 4.3 all-to-all-start.2
  93.3 35.9 %all-to-all-done.2 = bf16[16,18,2048]{2,1,0:T(8,128)(2,1)} async-done(((bf16[16,18,2048]{2,1,0:T(8,128)(2,1)}), bf16[16,18,2048]{2,1,0:T(8,128)(2,1)}, u32[]{:S(2)}, u32[]{:S(2)}) %all-to-all-start.2) | async-done | bytes 1179680 | tf_op jit(solution)/shard_map/all_to_all | solution.py:164
  129.1 4.5 all-to-all-start
  137.3 34.0 %all-to-all-done = bf16[16,18,2048]{2,1,0:T(8,128)(2,1)} async-done(((bf16[16,18,2048]{2,1,0:T(8,128)(2,1)}), bf16[16,18,2048]{2,1,0:T(8,128)(2,1)}, u32[]{:S(2)}, u32[]{:S(2)}) %all-to-all-start) | async-done | bytes 1179680 | tf_op jit(solution)/shard_map/all_to_all | solution.py:135
  173.9 8.1 %fusion.40 = f32[2,144,1536]{2,1,0:T(8,128)} fusion(bf16[2,2048,1536]{2,1,0:T(8,128)(2,1)} %all-gather.4.cloned.1.call-done, bf16[2,144,2048]{2,0,1:T(2,128)(2,1)S(1)} %bitcast.120), kind=kOutput, calls=%fused_computation.69 | convolution fusion | flops 1811939328 | bytes 15532032 | tf_op jit(solution)/shard_map/erd,edf->erf/dot_general | solution.py:140
  182.0 62.4 %all-gather.6.cloned.1.call-done = bf16[2,768,2048]{2,1,0:T(8,128)(2,1)} async-done(((bf16[2,192,2048]{2,1,0:T(8,128)(2,1)}), bf16[2,768,2048]{2,1,0:T(8,128)(2,1)}) %all-gather.6.cloned.1.call-update) | async-done | bytes 6291472 | tf_op jit(solution)/shard_map/all_gather | solution.py:138
  244.4 6.9 %multiply_convert_fusion.2 = (bf16[2,144,768]{2,1,0:T(8,128)(2,1)S(1)}, bf16[2,144,768]{2,1,0:T(8,128)(2,1)S(1)}, bf16[2,144,768]{2,1,0:T(8,128)(2,1)}) fusion(f32[2,144,1536]{2,1,0:T(8,128)} %fusion.40, bf16[2,768,2048]{2,1,0:T(8,128)(2,1)} %all-gather.6.cloned.1.call-done, bf16[2,144,2048]{2,0,1:T(2,128)(2,1)} %bitcast.122), kind=kOutput, calls=%fused_computation.75 | convolution fusion | flops 909508608 | bytes 10567680 | tf_op jit(solution)/shard_map/erd,efd->erf/dot_general | solution.py:166
  251.3 9.1 %convolution_convert_fusion.4 = bf16[2,144,2048]{2,1,0:T(8,128)(2,1)S(1)} fusion(bf16[2,2048,1536]{2,1,0:T(8,128)(2,1)} %all-gather.4.cloned.1.call-done, bf16[2,144,768]{2,1,0:T(8,128)(2,1)S(1)} %get-tuple-element.679, bf16[2,144,768]{2,1,0:T(8,128)(2,1)S(1)} %get-tuple-element.678), kind=kOutput, calls=%fused_computation.44 | convolution fusion | flops 1814298624 | bytes 14647296 | tf_op jit(solution)/shard_map/erf,edf->erd/dot_general | solution.py:179
  262.7 4.6 all-to-all-start.3
  273.5 23.2 %all-to-all-done.3 = bf16[2,144,2048]{2,0,1:T(2,128)(2,1)} async-done(((bf16[2,144,2048]{2,0,1:T(2,128)(2,1)}), bf16[2,144,2048]{2,0,1:T(2,128)(2,1)}, u32[]{:S(2)}, u32[]{:S(2)}) %all-to-all-start.3) | async-done | bytes 1179680 | tf_op jit(solution)/shard_map/all_to_all | solution.py:182
  309.5 20.9 %all-to-all-done.1 = bf16[2,144,2048]{2,0,1:T(2,128)(2,1)} async-done(((bf16[2,144,2048]{2,0,1:T(2,128)(2,1)}), bf16[2,144,2048]{2,0,1:T(2,128)(2,1)}, u32[]{:S(2)}, u32[]{:S(2)}) %all-to-all-start.1) | async-done | bytes 1179680 | tf_op jit(solution)/shard_map/all_to_all | solution.py:147
  345.5 20.3 %all-gather.8.cloned.1.call-done = bf16[256,2048]{1,0:T(8,128)(2,1)} async-done(((bf16[32,2048]{1,0:T(8,128)(2,1)}), bf16[256,2048]{1,0:T(8,128)(2,1)}) %all-gather.8.cloned.1.call-update) | async-done | bytes 1048592 | tf_op jit(solution)/shard_map/all_gather | solution.py:212
  369.1 6.0 convolution_convert_fusion.1
  375.2 7.8 %convolution_convert_fusion = bf16[2,2048,1536]{2,1,0:T(8,128)(2,1)} fusion(bf16[2,144,2048]{2,0,1:T(2,128)(2,1)S(1)} %bitcast.121, bf16[2,144,768]{2,1,0:T(8,128)(2,1)} %copy-done.13, bf16[2,144,768]{2,1,0:T(8,128)(2,1)} %copy-done.12), kind=kOutput, calls=%fused_computation.39 | convolution fusion | flops 1820000256 | bytes 14647296 | tf_op jit(solution)/shard_map/erd,erf->edf/dot_general | solution.py:176
  383.8 41.4 %psum.15 = f32[2048]{0:T(1024)} all-reduce(f32[2048]{0:T(1024)S(1)} %get-tuple-element.630), channel_id=1, replica_groups=mesh['ctx'=4,'exp'=8] {'ctx','exp'}, use_global_device_ids=true, to_apply=%region_32.33 | all-reduce | flops 2048 | bytes 16384 | tf_op jit(solution)/shard_map/psum | solution.py:207
  437.2 41.0 %reduce-scatter.11.cloned.1.call-done = bf16[2,192,2048]{2,1,0:T(8,128)(2,1)} async-done(((bf16[2,768,2048]{2,1,0:T(8,128)(2,1)}), bf16[2,192,2048]{2,1,0:T(8,128)(2,1)}) %reduce-scatter.11.cloned.1.call-update) | async-done | bytes 1572880 | tf_op jit(solution)/shard_map/reduce_scatter | solution.py:187
  481.7 120.6 %reduce-scatter.9.cloned.1.call-done = bf16[2,512,1536]{2,1,0:T(8,128)(2,1)} async-done(((bf16[2,2048,1536]{2,1,0:T(8,128)(2,1)}), bf16[2,512,1536]{2,1,0:T(8,128)(2,1)}) %reduce-scatter.9.cloned.1.call-update) | async-done | bytes 3145744 | tf_op jit(solution)/shard_map/reduce_scatter | solution.py:184
  602.4 5.5 convert_element_type.147
  607.8 6.3 %all-reduce.2.cloned.1.call-done = f32[2048,16]{0,1:T(8,128)} async-done(((f32[2048,16]{0,1:T(8,128)}), f32[2048,16]{0,1:T(8,128)}) %all-reduce.2.cloned.1.call-update) | async-done | bytes 131088 | tf_op jit(solution)/shard_map/psum | solution.py:207
  (162 shorter events, 93.4 us)
Async XLA Ops:
  8.0 33.4 %copy-start = (bf16[512,2048]{1,0:T(8,128)(2,1)S(1)}, bf16[512,2048]{1,0:T(8,128)(2,1)}, u32[]{:S(2)}) copy-start(bf16[512,2048]{1,0:T(8,128)(2,1)} %param.21) | copy-start | bytes 6291460
  8.0 72.9 %reduce-scatter.5.cloned.1.call-start = ((), (), s32[]{:S(2)}) async-start(), calls=%async_computation.8 | async-start | bytes 1179648 | tf_op jit(solution)/shard_map/reduce_scatter | solution.py:110
  14.3 7.9 %collective-permute-start = (bf16[256,256]{1,0:T(8,128)(2,1)}, bf16[256,256]{1,0:T(8,128)(2,1)S(1)}, u32[]{:S(2)}, u32[]{:S(2)}) collective-permute-start(bf16[256,256]{1,0:T(8,128)(2,1)} %get-tuple-element.827), channel_id=1, source_target_pairs={{0,8},{8,16},{16,24},{1,9},{9,17},{17,25},{2,10},{10,18},{18,26},{... | collective-permute-start | bytes 393224 | tf_op jit(solution)/shard_map/while/body/eval_jaxpr/ppermute | solution.py:21
  22.8 8.3 %collective-permute-start = (bf16[256,256]{1,0:T(8,128)(2,1)}, bf16[256,256]{1,0:T(8,128)(2,1)S(1)}, u32[]{:S(2)}, u32[]{:S(2)}) collective-permute-start(bf16[256,256]{1,0:T(8,128)(2,1)} %get-tuple-element.827), channel_id=1, source_target_pairs={{0,8},{8,16},{16,24},{1,9},{9,17},{17,25},{2,10},{10,18},{18,26},{... | collective-permute-start | bytes 393224 | tf_op jit(solution)/shard_map/while/body/eval_jaxpr/ppermute | solution.py:21
  31.8 7.1 %collective-permute-start = (bf16[256,256]{1,0:T(8,128)(2,1)}, bf16[256,256]{1,0:T(8,128)(2,1)S(1)}, u32[]{:S(2)}, u32[]{:S(2)}) collective-permute-start(bf16[256,256]{1,0:T(8,128)(2,1)} %get-tuple-element.827), channel_id=1, source_target_pairs={{0,8},{8,16},{16,24},{1,9},{9,17},{17,25},{2,10},{10,18},{18,26},{... | collective-permute-start | bytes 393224 | tf_op jit(solution)/shard_map/while/body/eval_jaxpr/ppermute | solution.py:21
  43.1 130.7 %all-gather.4.cloned.1.call-start = ((), (), s32[]{:S(2)}) async-start(), calls=%async_computation.9 | async-start | bytes 15728640 | tf_op jit(solution)/shard_map/all_gather | solution.py:137
  43.7 37.2 %copy-start.9 = (bf16[32,2048]{1,0:T(8,128)(2,1)S(1)}, bf16[32,2048]{1,0:T(8,128)(2,1)}, u32[]{:S(2)}) copy-start(bf16[32,2048]{1,0:T(8,128)(2,1)} %param.18) | copy-start | bytes 393220
  43.7 38.8 %copy-start.21 = (f32[2048]{0:T(1024)S(1)}, f32[2048]{0:T(1024)}, u32[]{:S(2)}) copy-start(f32[2048]{0:T(1024)} %param.22) | copy-start | bytes 24580
  43.8 39.8 %copy-start.19 = (bf16[2048,16]{0,1:T(8,128)(2,1)S(1)}, bf16[2048,16]{0,1:T(8,128)(2,1)}, u32[]{:S(2)}) copy-start(bf16[2048,16]{0,1:T(8,128)(2,1)} %param.23) | copy-start | bytes 196612
  43.8 200.7 %all-gather.6.cloned.1.call-start = ((), (), s32[]{:S(2)}) async-start(), calls=%async_computation.10 | async-start | bytes 7864320 | tf_op jit(solution)/shard_map/all_gather | solution.py:138
  44.7 39.3 %copy-start.15 = (f32[32,2048]{1,0:T(8,128)}, f32[32,2048]{1,0:T(8,128)S(1)}, u32[]{:S(2)}) copy-start(f32[32,2048]{1,0:T(8,128)S(1)} %convert_element_type.134) | copy-start | bytes 786436
  87.0 42.1 %all-to-all-start.2 = ((bf16[16,18,2048]{2,1,0:T(8,128)(2,1)}), bf16[16,18,2048]{2,1,0:T(8,128)(2,1)}, u32[]{:S(2)}, u32[]{:S(2)}) async-start(bf16[16,18,2048]{2,1,0:T(8,128)(2,1)} %reshape.252), calls=%async_computation.3 | async-start | bytes 3145728 | tf_op jit(solution)/shard_map/all_to_all | solution.py:164
  129.1 42.1 %all-to-all-start = ((bf16[16,18,2048]{2,1,0:T(8,128)(2,1)}), bf16[16,18,2048]{2,1,0:T(8,128)(2,1)}, u32[]{:S(2)}, u32[]{:S(2)}) async-start(bf16[16,18,2048]{2,1,0:T(8,128)(2,1)} %reshape.250), calls=%async_computation.1 | async-start | bytes 3145728 | tf_op jit(solution)/shard_map/all_to_all | solution.py:135
  262.7 34.1 %all-to-all-start.3 = ((bf16[2,144,2048]{2,0,1:T(2,128)(2,1)}), bf16[2,144,2048]{2,0,1:T(2,128)(2,1)}, u32[]{:S(2)}, u32[]{:S(2)}) async-start(bf16[2,144,2048]{2,0,1:T(2,128)(2,1)} %copy.162), calls=%async_computation.4 | async-start | bytes 2359296 | tf_op jit(solution)/shard_map/all_to_all | solution.py:182
  296.7 33.6 %all-to-all-start.1 = ((bf16[2,144,2048]{2,0,1:T(2,128)(2,1)}), bf16[2,144,2048]{2,0,1:T(2,128)(2,1)}, u32[]{:S(2)}, u32[]{:S(2)}) async-start(bf16[2,144,2048]{2,0,1:T(2,128)(2,1)} %copy.156), calls=%async_computation.2 | async-start | bytes 2359296 | tf_op jit(solution)/shard_map/all_to_all | solution.py:147
  301.0 64.8 %all-gather.8.cloned.1.call-start = ((), (), s32[]{:S(2)}) async-start(), calls=%async_computation.11 | async-start | bytes 1179648 | tf_op jit(solution)/shard_map/all_gather | solution.py:212
  338.9 26.9 %copy-start.8 = (bf16[256,4,128]{0,2,1:T(8,128)(2,1)S(1)}, bf16[256,4,128]{0,2,1:T(8,128)(2,1)}, u32[]{:S(2)}) copy-start(bf16[256,4,128]{0,2,1:T(8,128)(2,1)} %copy-done.7) | copy-start | bytes 786436
  345.5 89.5 %reduce-scatter.7.cloned.1.call-start = ((), (), s32[]{:S(2)}) async-start(), calls=%async_computation.12 | async-start | bytes 2621440 | tf_op jit(solution)/shard_map/reduce_scatter | solution.py:218
  369.1 109.2 %reduce-scatter.11.cloned.1.call-start = ((), (), s32[]{:S(2)}) async-start(), calls=%async_computation.14 | async-start | bytes 7864320 | tf_op jit(solution)/shard_map/reduce_scatter | solution.py:187
  375.2 227.2 %reduce-scatter.9.cloned.1.call-start = ((), (), s32[]{:S(2)}) async-start(), calls=%async_computation.13 | async-start | bytes 15728640 | tf_op jit(solution)/shard_map/reduce_scatter | solution.py:184
  383.1 42.1 %copy-start.11 = (bf16[32,2048]{1,0:T(8,128)(2,1)S(1)}, bf16[32,2048]{1,0:T(8,128)(2,1)}, u32[]{:S(2)}) copy-start(bf16[32,2048]{1,0:T(8,128)(2,1)} %copy-done.10) | copy-start | bytes 393220
  383.1 42.1 %copy-start.23 = (f32[32,16]{0,1:T(8,128)S(1)}, f32[32,16]{0,1:T(8,128)}, u32[]{:S(2)}) copy-start(f32[32,16]{0,1:T(8,128)} %copy-done.22) | copy-start | bytes 6148
  383.1 42.9 %copy-start.14 = (bf16[256,2048]{1,0:T(8,128)(2,1)S(1)}, bf16[256,2048]{1,0:T(8,128)(2,1)}, u32[]{:S(2)}) copy-start(bf16[256,2048]{1,0:T(8,128)(2,1)} %all-gather.8.cloned.1.call-done) | copy-start | bytes 3145732
  383.1 231.0 %all-reduce.2.cloned.1.call-start = ((), (), s32[]{:S(2)}) async-start(), calls=%async_computation.15 | async-start | bytes 262144 | tf_op jit(solution)/shard_map/psum | solution.py:207
  (19 other events, 54.4 us)
Sparse Core Ops, SparseCore 0:
  43.2 37.5 reduce-scatter.4
  345.6 20.1 all-gather.7
  426.1 187.8 all-reduce.1
Sparse Core Ops, SparseCore 1:
  45.5 127.2 all-gather.3
  174.5 69.9 all-gather.5
  369.2 34.8 reduce-scatter.6
  407.6 70.6 reduce-scatter.10
  481.4 120.9 reduce-scatter.8
where the time goes:
time: 625 us; the launch traced here: 623 us
  waiting for transfers between devices  411 us (66%)
  matrix products  62.4 us (10%)
  blocking collectives  41.4 us (7%)
  local copies, waits for them, and re-layouts  37.5 us (6%)
  starting transfers between devices  32.6 us (5%)
  other arithmetic  22.5 us (4%)
  between operations  16 us (3%)
    reduce_scatter x1, waiting for transfers between devices, per_device(): lax.psum_scatter(gate_up_term.astype(jnp.bfloat16), 'ctx', scatter_dimens...  121 us
    all_gather x1, waiting for transfers between devices, per_device(): lax.all_gather(expert_down, 'ctx', axis=1, tiled=True)  62.4 us
    psum x1, blocking collectives, per_device(): router_grad, gain_grad = lax.psum((router_term, gain_term), ('ctx', 'exp'))  41.4 us
    reduce_scatter x1, waiting for transfers between devices, per_device(): lax.psum_scatter(down_term.astype(jnp.bfloat16), 'ctx', scatter_dimension...  41 us
    reduce_scatter x1, waiting for transfers between devices, per_device(): lax.psum_scatter(jnp.dot(rows_here, out_weight, preferred_element_type=jn...  36.2 us
    all_to_all x1, waiting for transfers between devices, per_device(): lax.all_to_all(grad_outgoing, 'exp', split_axis=0, concat_axis=1, tiled=T...  35.9 us
    all_to_all x1, waiting for transfers between devices, per_device(): lax.all_to_all(outgoing, 'exp', split_axis=0, concat_axis=1, tiled=True)  34 us
    all_to_all x1, waiting for transfers between devices, per_device(): lax.all_to_all(rows_back, 'exp', split_axis=1, concat_axis=0, tiled=True)  23.2 us
  transfers between devices with their start and end apart: 15, of which 13 were waited for; matrix products, arithmetic and copies ran while one was open for 11% of the time, Pallas kernels for 0%

commit v1 on v0

v1 whole, which is shorter than its diff:
```python
import jax
import jax.numpy as jnp
from jax import lax
from jax.sharding import PartitionSpec as P

HEAD_WIDTH = 128
QUERY_HEADS = 32
KEY_VALUE_HEADS = 2
FFE = 768
EXPERTS = 16


norm_eps = 1e-06


def per_device(
    hidden_in,
    queries,
    keyvals,
    out_weight,
    norm_gain,
    router_weight,
    expert_gate_up,
    expert_down,
    route_ids,
    upstream,
):
    exp_count = lax.axis_size("exp")
    ctx_index = lax.axis_index("ctx")
    exp_index = lax.axis_index("exp")
    tok_ctx = queries.shape[0]
    tok_dev = hidden_in.shape[0]
    local_heads = queries.shape[1] // HEAD_WIDTH
    local_experts = EXPERTS // exp_count
    score_scale = HEAD_WIDTH ** (-0.5)

    keyvalue_head = exp_index * local_heads // (QUERY_HEADS // KEY_VALUE_HEADS)
    own_block = lax.dynamic_slice_in_dim(keyvals, keyvalue_head * 2 * HEAD_WIDTH, 2 * HEAD_WIDTH, 1)
    all_kv = lax.all_gather(own_block, "ctx", axis=0, tiled=True)
    ids_block = lax.all_gather(route_ids, "exp", axis=0, tiled=True)
    upstream_block = lax.all_gather(upstream, "exp", axis=0, tiled=True)
    gate_up_full = lax.all_gather(expert_gate_up, "ctx", axis=1, tiled=True)
    down_full = lax.all_gather(expert_down, "ctx", axis=1, tiled=True)
    upstream_all = lax.all_gather(upstream_block, "ctx", axis=0, tiled=True)

    keys, values = all_kv[:, :HEAD_WIDTH], all_kv[:, HEAD_WIDTH:]
    query_pos = ctx_index * tok_ctx + jnp.arange(tok_ctx, dtype=jnp.int32)
    key_pos = jnp.arange(keys.shape[0], dtype=jnp.int32)
    allowed = key_pos[None, :] <= query_pos[:, None]

    def columns(array, head):
        return array[:, head * HEAD_WIDTH : (head + 1) * HEAD_WIDTH]

    def dot_t(a, b):
        return lax.dot_general(a, b, (((1,), (1,)), ((), ())), preferred_element_type=jnp.float32)

    def head_scores(head):
        return jnp.where(allowed, dot_t(columns(queries, head), keys) * score_scale, -jnp.inf)

    attention_heads, log_totals = [], []
    for head in range(local_heads):
        scores = head_scores(head)
        row_max = jnp.max(scores, axis=1, keepdims=True)
        weights = jnp.exp(scores - row_max)
        row_sum = jnp.sum(weights, axis=1, keepdims=True)
        mixed = jnp.dot(weights.astype(jnp.bfloat16), values, preferred_element_type=jnp.float32)
        attention_heads.append((mixed / row_sum).astype(jnp.bfloat16))
        log_totals.append(row_max + jnp.log(row_sum))
    attention_flat = jnp.concatenate(attention_heads, axis=1)
    attention_all = lax.all_gather(attention_flat, "ctx", axis=0, tiled=True)

    projected = lax.psum_scatter(
        jnp.dot(attention_flat, out_weight, preferred_element_type=jnp.float32).astype(jnp.bfloat16),
        "exp",
        scatter_dimension=0,
        tiled=True,
    ).astype(jnp.float32)
    residual = hidden_in.astype(jnp.float32) + projected
    inv_rms = lax.rsqrt(jnp.mean(residual * residual, axis=1, keepdims=True) + norm_eps)
    normed = (residual * inv_rms * norm_gain).astype(jnp.bfloat16)

    normed_block = lax.all_gather(normed, "exp", axis=0, tiled=True)
    normed_cols = lax.all_to_all(normed_block, "ctx", split_axis=1, concat_axis=0, tiled=True)
    logits = jnp.dot(normed_block, router_weight, preferred_element_type=jnp.float32)
    expert_ids = jnp.arange(EXPERTS, dtype=jnp.int32)
    hit_block = jnp.any(ids_block[:, :, None] == expert_ids, axis=1)
    masked = jnp.where(hit_block, logits, -jnp.inf)
    shifted = jnp.exp(masked - jnp.max(masked, axis=1, keepdims=True))
    probs_block = shifted / jnp.sum(shifted, axis=1, keepdims=True)
    probs_here = lax.dynamic_slice_in_dim(probs_block, exp_index * local_experts, local_experts, 1)
    probs_cols = probs_here.T[:, :, None]
    out_grad_block = upstream_block.astype(jnp.float32)
    row_grads = (probs_cols * out_grad_block[None]).astype(jnp.bfloat16)

    gate_up = jnp.einsum("td,edf->etf", normed_block, gate_up_full, preferred_element_type=jnp.float32)
    gate_part = gate_up[:, :, :FFE]
    up_part = gate_up[:, :, FFE:]
    sigmoid_gate = jax.nn.sigmoid(gate_part)
    activation = (gate_part * sigmoid_gate * up_part).astype(jnp.bfloat16)
    scaled_act = (probs_cols * activation.astype(jnp.float32)).astype(jnp.bfloat16)
    act_grad = jnp.einsum("etd,efd->etf", row_grads, down_full, preferred_element_type=jnp.float32)
    gate_grad = act_grad * up_part * sigmoid_gate * (1.0 + gate_part * (1.0 - sigmoid_gate))
    up_grad = act_grad * gate_part * sigmoid_gate
    pair_grad = jnp.concatenate([gate_grad, up_grad], axis=2).astype(jnp.bfloat16)
    pair_grad_all = lax.all_gather(pair_grad, "ctx", axis=1, tiled=True)
    rows_back = jnp.einsum("etf,edf->td", pair_grad, gate_up_full, preferred_element_type=jnp.float32)
    expert_part = lax.psum_scatter(
        rows_back.astype(jnp.bfloat16), "exp", scatter_dimension=0, tiled=True
    ).astype(jnp.float32)

    expert_out = jnp.einsum(
        "etf,efd->etd", activation, down_full, preferred_element_type=jnp.float32
    ).astype(jnp.bfloat16).astype(jnp.float32)
    prob_grads_here = jnp.sum(expert_out * out_grad_block[None], axis=2)
    prob_grads = lax.all_to_all(
        prob_grads_here, "exp", split_axis=1, concat_axis=0, tiled=True
    ).T
    mixture = lax.psum_scatter(
        jnp.sum(probs_cols * expert_out, axis=0).astype(jnp.bfloat16),
        "exp",
        scatter_dimension=0,
        tiled=True,
    ).astype(jnp.float32)
    layer_out = (residual + mixture).astype(jnp.bfloat16)

    act_rows = lax.all_to_all(
        jnp.swapaxes(scaled_act, 1, 2), "ctx", split_axis=1, concat_axis=2, tiled=True
    )
    down_grad = jnp.einsum("eft,td->efd", act_rows, upstream_all, preferred_element_type=jnp.float32)
    gate_up_grad = jnp.einsum(
        "td,etf->edf", normed_cols, pair_grad_all, preferred_element_type=jnp.float32
    )

    out_grad = upstream.astype(jnp.float32)
    probs = lax.dynamic_slice_in_dim(probs_block, exp_index * tok_dev, tok_dev, 0)
    logit_grad = probs * (prob_grads - jnp.sum(probs * prob_grads, axis=1, keepdims=True))
    router_term = jnp.einsum(
        "te,td->ed", logit_grad, normed.astype(jnp.float32), precision=lax.Precision.HIGHEST
    )
    normed_grad = expert_part + jnp.einsum(
        "te,de->td", logit_grad, router_weight.astype(jnp.float32), precision=lax.Precision.HIGHEST
    )
    gain_term = jnp.sum(normed_grad * residual * inv_rms, axis=0, keepdims=True)
    summed = lax.psum(jnp.concatenate([router_term, gain_term], axis=0), ("ctx", "exp"))
    router_grad, gain_grad = summed[:EXPERTS].T, summed[EXPERTS]
    inner_mean = jnp.mean(residual * norm_gain * normed_grad, axis=1, keepdims=True)
    input_grad = (
        out_grad + norm_gain * inv_rms * normed_grad - residual * inv_rms**3 * inner_mean
    ).astype(jnp.bfloat16)

    arriving = lax.all_gather(input_grad, "exp", axis=0, tiled=True)
    arriving_cols = lax.all_to_all(arriving, "ctx", split_axis=1, concat_axis=0, tiled=True)
    out_weight_grad = jnp.einsum(
        "tc,td->cd", attention_all, arriving_cols, preferred_element_type=jnp.float32
    )
    attention_grad = dot_t(arriving, out_weight).astype(jnp.bfloat16)

    query_grads = []
    for head in range(local_heads):
        grad_head = columns(attention_grad, head)
        delta = jnp.sum(
            grad_head.astype(jnp.float32) * attention_heads[head].astype(jnp.float32),
            axis=1,
            keepdims=True,
        )
        attn_probs = jnp.exp(head_scores(head) - log_totals[head])
        score_grad = (attn_probs * (dot_t(grad_head, values) - delta)).astype(jnp.bfloat16)
        query_acc = jnp.dot(score_grad, keys, preferred_element_type=jnp.float32)
        query_grads.append((score_scale * query_acc).astype(jnp.bfloat16))
    query_grad = jnp.concatenate(query_grads, axis=1)
    return (
        layer_out,
        input_grad,
        query_grad,
        out_weight_grad,
        gate_up_grad,
        down_grad,
        router_grad,
        gain_grad,
    )


def solution(mesh):
    return jax.shard_map(
        per_device,
        mesh=mesh,
        in_specs=(
            P(("ctx", "exp"), None),
            P("ctx", "exp"),
            P("ctx", None),
            P("exp", None),
            P(),
            P(),
            P("exp", "ctx", None),
            P("exp", "ctx", None),
            P(("ctx", "exp"), None),
            P(("ctx", "exp"), None),
        ),
        out_specs=(
            P(("ctx", "exp"), None),
            P(("ctx", "exp"), None),
            P("ctx", "exp"),
            P("exp", "ctx"),
            P("exp", "ctx", None),
            P("exp", "ctx", None),
            P(),
            P(),
        ),
        check_vma=False,
    )
```

time: 625 us -> 747 us (1.20)
  waiting for transfers between devices: 411 us -> 573 us
  local copies, waits for them, and re-layouts: 37.5 us -> 21.9 us
  blocking collectives: 41.4 us -> 25.9 us
  starting transfers between devices: 32.6 us -> 18.1 us
  matrix products: 62.4 us -> 74 us
    all_gather x2 -> x7, waiting for transfers between devices: 62.5 us -> 318 us  [the longest x1 122 us: per_device(): gate_up_full = lax.all_gather(expert_gate_up, 'ctx', axis=1, tiled=True)]
    reduce_scatter x4 -> x3, waiting for transfers between devices: 198 us -> 75.3 us  [the longest x1 32.2 us: per_device(): lax.psum_scatter(jnp.dot(attention_flat, out_weight, preferred_element_ty...]
    psum x1, waiting for transfers between devices: 6.25 us -> 125 us  [per_device(): lax.psum(jnp.concatenate([router_term, gain_term], axis=0), ('ctx', 'exp'))]
    all_to_all x4, waiting for transfers between devices: 114 us -> 29.7 us  [the longest x1 13.4 us: per_device(): lax.all_to_all(jnp.swapaxes(scaled_act, 1, 2), 'ctx', split_axis=1, conca...]
    psum x1 -> x0, blocking collectives: 41.4 us -> none  [per_device(): router_grad, gain_grad = lax.psum((router_term, gain_term), ('ctx', 'exp'))]
    all_gather x0 -> x2, blocking collectives: none -> 25.9 us  [the longest x1 14.4 us: per_device(): ids_block = lax.all_gather(route_ids, 'exp', axis=0, tiled=True)]
    ppermute x3 -> x0, starting transfers between devices: 14.6 us -> none  [from_behind(): return lax.ppermute(shard, axis, pairs)]
    dot_general x18 -> x23, matrix products: 60.8 us -> 72.5 us  [the longest x1 9.98 us: per_device(): jnp.einsum('td,edf->etf', normed_block, gate_up_full, preferred_element_t...]
  transfers between devices with their start and end apart: 15 -> 16, of which waited for: 13 -> 15; matrix products, arithmetic and copies ran while one was open for 11% -> 9% of each run, Pallas kernels for 0% -> 0%
where the time goes in v1:
time: 747 us; the launch traced here: 746 us
  waiting for transfers between devices  573 us (77%)
  matrix products  74 us (10%)
  blocking collectives  25.9 us (3%)
  local copies, waits for them, and re-layouts  21.9 us (3%)
  other arithmetic  18.3 us (2%)
  starting transfers between devices  18.1 us (2%)
  between operations  14.8 us (2%)
    psum x1, waiting for transfers between devices, per_device(): lax.psum(jnp.concatenate([router_term, gain_term], axis=0), ('ctx', 'exp'))  125 us
    all_gather x1, waiting for transfers between devices, per_device(): gate_up_full = lax.all_gather(expert_gate_up, 'ctx', axis=1, tiled=True)  122 us
    all_gather x1, waiting for transfers between devices, per_device(): pair_grad_all = lax.all_gather(pair_grad, 'ctx', axis=1, tiled=True)  68.7 us
    all_gather x1, waiting for transfers between devices, per_device(): down_full = lax.all_gather(expert_down, 'ctx', axis=1, tiled=True)  61.8 us
    reduce_scatter x1, waiting for transfers between devices, per_device(): lax.psum_scatter(jnp.dot(attention_flat, out_weight, preferred_element_ty...  32.2 us
    reduce_scatter x1, waiting for transfers between devices, per_device(): lax.psum_scatter(jnp.sum(probs_cols * expert_out, axis=0).astype(jnp.bflo...  30.1 us
    all_gather x1, waiting for transfers between devices, per_device(): upstream_all = lax.all_gather(upstream_block, 'ctx', axis=0, tiled=True)  29.4 us
    all_gather x1, waiting for transfers between devices, per_device(): arriving = lax.all_gather(input_grad, 'exp', axis=0, tiled=True)  22.2 us
  transfers between devices with their start and end apart: 16, of which 15 were waited for; matrix products, arithmetic and copies ran while one was open for 9% of the time, Pallas kernels for 0%

profile of v1, /device:TPU:0, one launch (start us, length us, event | category | flops | bytes accessed | tf_op | source)
XLA Modules:
  0.0 746.0 jit_solution(9986827355923564355)
XLA Ops:
  8.3 11.5 %all_gather.30 = bf16[1024,256]{1,0:T(8,128)(2,1)S(1)} all-gather(bf16[256,256]{1,0:T(8,128)(2,1)S(1)} %constant_dynamic-slice_fusion), channel_id=1, replica_groups=mesh['ctx'=4,'exp'=8] {'ctx'}, dimensions={0}, use_global_device_ids=true | all-gather | bytes 655360 | tf_op jit(solution)/shard_map/all_gather | solution.py:39
  28.3 32.2 %reduce-scatter.4.cloned.1.call-done = bf16[32,2048]{1,0:T(8,128)(2,1)} async-done(((bf16[256,2048]{1,0:T(8,128)(2,1)}), bf16[32,2048]{1,0:T(8,128)(2,1)}) %reduce-scatter.4.cloned.1.call-update) | async-done | bytes 131088 | tf_op jit(solution)/shard_map/reduce_scatter | solution.py:72
  65.1 14.4 %all-gather = s32[8,32,8]{1,2,0:T(8,128)S(1)} all-gather(s32[1,32,8]{1,2,0:T(8,128)S(1)} %bitcast.93), channel_id=1, replica_groups=mesh['ctx'=4,'exp'=8] {'exp'}, dimensions={0}, use_global_device_ids=true | all-gather | bytes 9216 | tf_op jit(solution)/shard_map/all_gather | solution.py:40
  85.3 21.3 %all-gather.10.cloned.1.call-done = bf16[256,2048]{1,0:T(8,128)(2,1)} async-done(((bf16[32,2048]{1,0:T(8,128)(2,1)}), bf16[256,2048]{1,0:T(8,128)(2,1)}) %all-gather.10.cloned.1.call-update) | async-done | bytes 1048592 | tf_op jit(solution)/shard_map/all_gather | solution.py:82
  108.3 122.0 %all-gather.12.cloned.1.call-done = bf16[2,2048,1536]{2,1,0:T(8,128)(2,1)} async-done(((bf16[2,512,1536]{2,1,0:T(8,128)(2,1)}), bf16[2,2048,1536]{2,1,0:T(8,128)(2,1)}) %all-gather.12.cloned.1.call-update) | async-done | bytes 12582928 | tf_op jit(solution)/shard_map/all_gather | solution.py:42
  230.4 10.0 %convolution_bitcast_fusion.1 = f32[2,256,1536]{2,1,0:T(8,128)} fusion(bf16[2,2048,1536]{2,1,0:T(8,128)(2,1)} %all-gather.12.cloned.1.call-done, bf16[256,2048]{1,0:T(8,128)(2,1)} %all-gather.10.cloned.1.call-done), kind=kOutput, calls=%fused_computation.8 | convolution fusion | flops 3221225472 | bytes 16777216 | tf_op jit(solution)/shard_map/td,edf->etf/dot_general | solution.py:95
  240.3 61.8 %all-gather.14.cloned.1.call-done = bf16[2,768,2048]{2,1,0:T(8,128)(2,1)} async-done(((bf16[2,192,2048]{2,1,0:T(8,128)(2,1)}), bf16[2,768,2048]{2,1,0:T(8,128)(2,1)}) %all-gather.14.cloned.1.call-update) | async-done | bytes 6291472 | tf_op jit(solution)/shard_map/all_gather | solution.py:43
  302.1 9.5 %multiply_convert_fusion.4 = (bf16[2,256,768]{2,1,0:T(8,128)(2,1)S(1)}, bf16[2,256,768]{2,1,0:T(8,128)(2,1)S(1)}, bf16[2,768,256]{1,2,0:T(8,128)(2,1)}, bf16[2,256,768]{2,1,0:T(8,128)(2,1)}) fusion(f32[2,256,1536]{2,1,0:T(8,128)} %convolution_bitcast_fusion.1, f32[2,256]{1,0:T(2,128)S(1)} %dynamic-slice_bitcast_fusion, ...), kind=kOutput, calls=%fused_computation.20 | convolution fusion | flops 1620180992 | bytes 14684160 | tf_op jit(solution)/shard_map/etd,efd->etf/dot_general | solution.py:101
  312.4 9.0 %fusion.4 = bf16[256,2048]{1,0:T(8,128)(2,1)} fusion(bf16[2,2048,1536]{2,1,0:T(8,128)(2,1)} %all-gather.12.cloned.1.call-done, bf16[2,256,768]{2,1,0:T(8,128)(2,1)S(1)} %get-tuple-element.51, bf16[2,256,768]{2,1,0:T(8,128)(2,1)S(1)} %get-tuple-element.50), kind=kOutput, calls=%fused_computation.12 | convolution fusion | flops 3224895488 | bytes 15204352 | tf_op jit(solution)/shard_map/etf,edf->td/dot_general | solution.py:106
  321.5 7.0 fusion.1
  329.9 4.6 all-to-all-start
  334.6 5.6 all-to-all-done
  341.2 13.0 %reduce-scatter.8.cloned.1.call-done = bf16[32,2048]{1,0:T(8,128)(2,1)} async-done(((bf16[256,2048]{1,0:T(8,128)(2,1)}), bf16[32,2048]{1,0:T(8,128)(2,1)}) %reduce-scatter.8.cloned.1.call-update) | async-done | bytes 131088 | tf_op jit(solution)/shard_map/reduce_scatter | solution.py:107
  357.9 30.1 %reduce-scatter.6.cloned.1.call-done = bf16[32,2048]{1,0:T(8,128)(2,1)} async-done(((bf16[256,2048]{1,0:T(8,128)(2,1)}), bf16[32,2048]{1,0:T(8,128)(2,1)}) %reduce-scatter.6.cloned.1.call-update) | async-done | bytes 131088 | tf_op jit(solution)/shard_map/reduce_scatter | solution.py:118
  405.0 13.4 %all-to-all-done.3 = bf16[2,768,256]{2,0,1:T(2,128)(2,1)} async-done(((bf16[2,768,256]{2,0,1:T(2,128)(2,1)}), bf16[2,768,256]{2,0,1:T(2,128)(2,1)}, u32[]{:S(2)}, u32[]{:S(2)}) %all-to-all-start.3) | async-done | bytes 786464 | tf_op jit(solution)/shard_map/all_to_all | solution.py:126
  419.7 29.4 %all-gather.24.cloned.1.call-done = bf16[1024,2048]{1,0:T(8,128)(2,1)} async-done(((bf16[256,2048]{1,0:T(8,128)(2,1)}), bf16[1024,2048]{1,0:T(8,128)(2,1)}) %all-gather.24.cloned.1.call-update) | async-done | bytes 4194320 | tf_op jit(solution)/shard_map/all_gather | solution.py:44
  449.1 5.6 fusion.2
  454.8 125.2 %all-reduce.2.cloned.1.call-done = f32[17,2048]{1,0:T(8,128)} async-done(((f32[17,2048]{1,0:T(8,128)}), f32[17,2048]{1,0:T(8,128)}) %all-reduce.2.cloned.1.call-update) | async-done | bytes 139280 | tf_op jit(solution)/shard_map/psum | solution.py:144
  583.0 22.2 %all-gather.18.cloned.1.call-done = bf16[256,2048]{1,0:T(8,128)(2,1)} async-done(((bf16[32,2048]{1,0:T(8,128)(2,1)}), bf16[256,2048]{1,0:T(8,128)(2,1)}) %all-gather.18.cloned.1.call-update) | async-done | bytes 1048592 | tf_op jit(solution)/shard_map/all_gather | solution.py:151
  618.2 10.8 %all-to-all-done.1 = bf16[256,4,512]{2,0,1:T(8,128)(2,1)} async-done(((bf16[256,4,512]{2,0,1:T(8,128)(2,1)}), bf16[256,4,512]{2,0,1:T(8,128)(2,1)}, u32[]{:S(2)}, u32[]{:S(2)}) %all-to-all-start.1) | async-done | bytes 1048608 | tf_op jit(solution)/shard_map/all_to_all | solution.py:152
  639.8 11.8 %all-gather.20.cloned.1.call-done = bf16[1024,512]{0,1:T(8,128)(2,1)} async-done(((bf16[256,512]{0,1:T(8,128)(2,1)}), bf16[1024,512]{0,1:T(8,128)(2,1)}) %all-gather.20.cloned.1.call-update) | async-done | bytes 1048592 | tf_op jit(solution)/shard_map/all_gather | solution.py:70
  654.8 68.7 %all-gather.22.cloned.1.call-done = bf16[2,1024,1536]{2,1,0:T(8,128)(2,1)} async-done(((bf16[2,256,1536]{2,1,0:T(8,128)(2,1)}), bf16[2,1024,1536]{2,1,0:T(8,128)(2,1)}) %all-gather.22.cloned.1.call-update) | async-done | bytes 6291472 | tf_op jit(solution)/shard_map/all_gather | solution.py:105
  723.5 9.1 %convolution_bitcast_fusion = f32[2,512,1536]{1,2,0:T(8,128)} fusion(bf16[2,1024,1536]{2,1,0:T(8,128)(2,1)} %all-gather.22.cloned.1.call-done, bf16[1024,512,1]{1,0,2:T(8,128)(2,1)} %bitcast.18), kind=kOutput, calls=%fused_computation.2 | convolution fusion | flops 3221225472 | bytes 13631488 | tf_op jit(solution)/shard_map/td,etf->edf/dot_general | solution.py:130
  732.6 6.6 copy.65
  (171 shorter events, 76.5 us)
Async XLA Ops:
  7.2 53.3 %reduce-scatter.4.cloned.1.call-start = ((), (), s32[]{:S(2)}) async-start(), calls=%async_computation.7 | async-start | bytes 1179648 | tf_op jit(solution)/shard_map/reduce_scatter | solution.py:72
  25.4 35.1 %copy-start.2 = (bf16[32,2048]{1,0:T(8,128)(2,1)S(1)}, bf16[32,2048]{1,0:T(8,128)(2,1)}, u32[]{:S(2)}) copy-start(bf16[32,2048]{1,0:T(8,128)(2,1)} %param.10) | copy-start | bytes 393220
  25.4 36.8 %copy-start.21 = (f32[2048]{0:T(1024)S(1)}, f32[2048]{0:T(1024)}, u32[]{:S(2)}) copy-start(f32[2048]{0:T(1024)} %param.14) | copy-start | bytes 24580
  25.8 38.7 %copy-start.14 = (bf16[256,128]{0,1:T(8,128)(2,1)}, bf16[256,128]{0,1:T(8,128)(2,1)S(1)}, u32[]{:S(2)}) copy-start(bf16[256,128]{0,1:T(8,128)(2,1)S(1)} %fusion.35) | copy-start | bytes 196612
  27.5 37.6 %copy-start.24 = (s32[32,8]{0,1:T(8,128)S(1)}, s32[32,8]{0,1:T(8,128)}, u32[]{:S(2)}) copy-start(s32[32,8]{0,1:T(8,128)} %param.18) | copy-start | bytes 3076
  27.5 55.0 %all-gather.16.cloned.1.call-start = ((), (), s32[]{:S(2)}) async-start(), calls=%async_computation.12 | async-start | bytes 1179648 | tf_op jit(solution)/shard_map/all_gather | solution.py:41
  28.3 78.4 %all-gather.10.cloned.1.call-start = ((), (), s32[]{:S(2)}) async-start(), calls=%async_computation.8 | async-start | bytes 1179648 | tf_op jit(solution)/shard_map/all_gather | solution.py:82
  63.9 166.5 %all-gather.12.cloned.1.call-start = ((), (), s32[]{:S(2)}) async-start(), calls=%async_computation.9 | async-start | bytes 15728640 | tf_op jit(solution)/shard_map/all_gather | solution.py:42
  64.5 42.2 %copy-start.19 = (bf16[2048,16]{0,1:T(8,128)(2,1)S(1)}, bf16[2048,16]{0,1:T(8,128)(2,1)}, u32[]{:S(2)}) copy-start(bf16[2048,16]{0,1:T(8,128)(2,1)} %param.15) | copy-start | bytes 196612
  64.5 237.6 %all-gather.14.cloned.1.call-start = ((), (), s32[]{:S(2)}) async-start(), calls=%async_computation.10 | async-start | bytes 7864320 | tf_op jit(solution)/shard_map/all_gather | solution.py:43
  65.1 289.1 %reduce-scatter.8.cloned.1.call-start = ((), (), s32[]{:S(2)}) async-start(), calls=%async_computation.13 | async-start | bytes 1179648 | tf_op jit(solution)/shard_map/reduce_scatter | solution.py:107
  108.3 231.9 %copy-start.20 = (f32[256,16]{0,1:T(8,128)}, f32[256,16]{0,1:T(8,128)S(1)}, u32[]{:S(2)}) copy-start(f32[256,16]{0,1:T(8,128)S(1)} %fusion.107) | copy-start | bytes 49156
  321.4 66.6 %reduce-scatter.6.cloned.1.call-start = ((), (), s32[]{:S(2)}) async-start(), calls=%async_computation.11 | async-start | bytes 1179648 | tf_op jit(solution)/shard_map/reduce_scatter | solution.py:118
  321.5 32.7 %copy-start.3 = (bf16[32,2048]{1,0:T(8,128)(2,1)S(1)}, bf16[32,2048]{1,0:T(8,128)(2,1)}, u32[]{:S(2)}) copy-start(bf16[32,2048]{1,0:T(8,128)(2,1)} %reduce-scatter.4.cloned.1.call-done) | copy-start | bytes 393220
  328.5 120.6 %all-gather.24.cloned.1.call-start = ((), (), s32[]{:S(2)}) async-start(), calls=%async_computation.17 | async-start | bytes 5242880 | tf_op jit(solution)/shard_map/all_gather | solution.py:44
  329.9 10.2 %all-to-all-start = ((f32[2,8,32]{2,0,1:T(2,128)}), f32[2,8,32]{2,0,1:T(2,128)S(1)}, u32[]{:S(2)}, u32[]{:S(2)}) async-start(f32[2,8,32]{2,0,1:T(2,128)} %copy.52), calls=%async_computation.3 | async-start | bytes 16384 | tf_op jit(solution)/shard_map/all_to_all | solution.py:115
  334.5 245.4 %all-reduce.2.cloned.1.call-start = ((), (), s32[]{:S(2)}) async-start(), calls=%async_computation.18 | async-start | bytes 393216 | tf_op jit(solution)/shard_map/psum | solution.py:144
  357.9 247.3 %all-gather.18.cloned.1.call-start = ((), (), s32[]{:S(2)}) async-start(), calls=%async_computation.14 | async-start | bytes 1179648 | tf_op jit(solution)/shard_map/all_gather | solution.py:151
  389.9 261.7 %all-gather.20.cloned.1.call-start = ((), (), s32[]{:S(2)}) async-start(), calls=%async_computation.15 | async-start | bytes 1310720 | tf_op jit(solution)/shard_map/all_gather | solution.py:70
  391.5 332.0 %all-gather.22.cloned.1.call-start = ((), (), s32[]{:S(2)}) async-start(), calls=%async_computation.16 | async-start | bytes 7864320 | tf_op jit(solution)/shard_map/all_gather | solution.py:105
  397.7 20.7 %all-to-all-start.3 = ((bf16[2,768,256]{2,0,1:T(2,128)(2,1)}), bf16[2,768,256]{2,0,1:T(2,128)(2,1)}, u32[]{:S(2)}, u32[]{:S(2)}) async-start(bf16[2,768,256]{2,0,1:T(2,128)(2,1)} %copy.61), calls=%async_computation.6 | async-start | bytes 1572864 | tf_op jit(solution)/shard_map/all_to_all | solution.py:126
  607.5 21.6 %all-to-all-start.1 = ((bf16[256,4,512]{2,0,1:T(8,128)(2,1)}), bf16[256,4,512]{2,0,1:T(8,128)(2,1)}, u32[]{:S(2)}, u32[]{:S(2)}) async-start(bf16[256,4,512]{2,0,1:T(8,128)(2,1)} %bitcast.83), calls=%async_computation.4 | async-start | bytes 2097152 | tf_op jit(solution)/shard_map/all_to_all | solution.py:152
  616.2 19.6 %copy-start.6 = (f32[256,1024]{0,1:T(8,128)S(1)}, f32[256,1024]{0,1:T(8,128)}, u32[]{:S(2)}) copy-start(f32[256,1024]{0,1:T(8,128)} %copy-done.5) | copy-start | bytes 3145732
  629.0 25.8 %all-to-all-start.2 = ((bf16[256,4,512]{2,0,1:T(8,128)(2,1)}), bf16[256,4,512]{2,0,1:T(8,128)(2,1)}, u32[]{:S(2)}, u32[]{:S(2)}) async-start(bf16[256,4,512]{2,0,1:T(8,128)(2,1)} %bitcast.82), calls=%async_computation.5 | async-start | bytes 2097152 | tf_op jit(solution)/shard_map/all_to_all | solution.py:83
  (35 other events, 233.9 us)
Sparse Core Ops, SparseCore 0:
  27.6 32.8 reduce-scatter.3
  62.1 20.3 all-gather.15
  84.7 21.9 all-gather.9
  108.3 121.9 all-gather.11
  232.0 70.0 all-gather.13
  321.6 32.5 reduce-scatter.7
  357.0 30.9 reduce-scatter.5
  389.9 59.2 all-gather.23
  455.3 124.6 all-reduce.1
  582.0 23.1 all-gather.17
  607.0 44.5 all-gather.19
  653.9 69.5 all-gather.21

commit v2 on v0

--- a/solution.py
+++ b/solution.py
@@ -13,12 +13,6 @@
 
 
 norm_eps = 1e-06
-
-
-def from_behind(shard, axis, by):
-    count = lax.axis_size(axis)
-    pairs = [(i, i + by) for i in range(count) if 0 <= i + by < count]
-    return lax.ppermute(shard, axis, pairs)
 
 
 def per_device(
@@ -41,71 +35,31 @@
     score_scale = HEAD_WIDTH ** (-0.5)
     keyvalue_head = expert_number * local_heads // (QUERY_HEADS // KEY_VALUE_HEADS)
     own_block = lax.dynamic_slice_in_dim(keyvals, keyvalue_head * 2 * HEAD_WIDTH, 2 * HEAD_WIDTH, 1)
-    query_heads = queries.reshape(tok_ctx, local_heads, HEAD_WIDTH)
+    all_kv = lax.all_gather(own_block, "ctx", axis=0, tiled=True)
+    keys, values = all_kv[:, :HEAD_WIDTH], all_kv[:, HEAD_WIDTH:]
     query_pos = ctx_index * tok_ctx + jnp.arange(tok_ctx, dtype=jnp.int32)
-    key_offsets = jnp.arange(tok_ctx, dtype=jnp.int32)
-
-    def block_scores(kv_block, anchor):
-        scores = (
-            jnp.einsum(
-                "qhd,kd->qhk",
-                query_heads,
-                kv_block[:, :HEAD_WIDTH],
-                preferred_element_type=jnp.float32,
-            )
-            * score_scale
-        )
-        allowed = (anchor * tok_ctx + key_offsets)[None, :] <= query_pos[:, None]
-        return jnp.where(allowed[:, None, :], scores, -jnp.inf)
-
-    def absorb(running, kv_block, anchor):
-        row_max, row_sum, mixed = running
-        scores = block_scores(kv_block, anchor)
-        new_max = jnp.maximum(row_max, jnp.max(scores, axis=2))
-        weights = jnp.exp(scores - new_max[:, :, None])
-        decay_factor = jnp.exp(row_max - new_max)
-        row_sum = row_sum * decay_factor + jnp.sum(weights, axis=2)
-        mixed = mixed * decay_factor[:, :, None] + jnp.einsum(
-            "qhk,kd->qhd",
-            weights.astype(jnp.bfloat16),
-            kv_block[:, HEAD_WIDTH:],
-            preferred_element_type=jnp.float32,
-        )
-        return (new_max, row_sum, mixed)
-
-    start_running = (
-        jnp.full((tok_ctx, local_heads), -jnp.inf, jnp.float32),
-        jnp.zeros((tok_ctx, local_heads), jnp.float32),
-        jnp.zeros((tok_ctx, local_heads, HEAD_WIDTH), jnp.float32),
-    )
-    running = absorb(start_running, own_block, ctx_index)
-    stored = jnp.zeros((ctx_count, tok_ctx, 2 * HEAD_WIDTH), own_block.dtype)
-    stored = lax.dynamic_update_index_in_dim(stored, own_block, ctx_index, 0)
-
-    def forward_step(hop_count, loop_state):
-        kv_block, running, stored = loop_state
-        kv_block = from_behind(kv_block, "ctx", 1)
-        anchor = ctx_index - hop_count
-
-        def use_block():
-            return (
-                absorb(running, kv_block, anchor),
-                lax.dynamic_update_index_in_dim(stored, kv_block, anchor, 0),
-            )
-
-        def skip_block():
-            return (running, stored)
-
-        running, stored = lax.cond(hop_count <= ctx_index, use_block, skip_block)
-        return (kv_block, running, stored)
-
-    final_block, running, stored = lax.fori_loop(
-        1, ctx_count, forward_step, (own_block, running, stored)
-    )
-    row_max, row_sum, mixed = running
-    attention = (mixed / row_sum[:, :, None]).astype(jnp.bfloat16)
-    log_total = row_max + jnp.log(row_sum)
-    attention_flat = attention.reshape(tok_ctx, local_heads * HEAD_WIDTH)
+    key_pos = jnp.arange(keys.shape[0], dtype=jnp.int32)
+    allowed = key_pos[None, :] <= query_pos[:, None]
+
+    def columns(array, head):
+        return array[:, head * HEAD_WIDTH : (head + 1) * HEAD_WIDTH]
+
+    def dot_t(a, b):
+        return lax.dot_general(a, b, (((1,), (1,)), ((), ())), preferred_element_type=jnp.float32)
+
+    def head_scores(head):
+        return jnp.where(allowed, dot_t(columns(queries, head), keys) * score_scale, -jnp.inf)
+
+    attention_heads, log_totals = [], []
+    for head in range(local_heads):
+        scores = head_scores(head)
+        row_max = jnp.max(scores, axis=1, keepdims=True)
+        weights = jnp.exp(scores - row_max)
+        row_sum = jnp.sum(weights, axis=1, keepdims=True)
+        mixed = jnp.dot(weights.astype(jnp.bfloat16), values, preferred_element_type=jnp.float32)
+        attention_heads.append((mixed / row_sum).astype(jnp.bfloat16))
+        log_totals.append(row_max + jnp.log(row_sum))
+    attention_flat = jnp.concatenate(attention_heads, axis=1)
     rows_here = attention_flat
     projected = lax.psum_scatter(
         jnp.dot(rows_here, out_weight, preferred_element_type=jnp.float32).astype(jnp.bfloat16),
@@ -199,12 +153,13 @@
     )
     logit_grad = jnp.sum(jnp.where(expert_hit, chosen_grad[:, :, None], 0.0), axis=1)
     normed_float = normed.astype(jnp.float32)
-    router_term = jnp.einsum("td,te->de", normed_float, logit_grad, precision=lax.Precision.HIGHEST)
+    router_term = jnp.einsum("te,td->ed", logit_grad, normed_float, precision=lax.Precision.HIGHEST)
     normed_grad = expert_part + jnp.einsum(
         "te,de->td", logit_grad, router_weight.astype(jnp.float32), precision=lax.Precision.HIGHEST
     )
-    gain_term = jnp.sum(normed_grad * residual * inv_rms, axis=0)
-    router_grad, gain_grad = lax.psum((router_term, gain_term), ("ctx", "exp"))
+    gain_term = jnp.sum(normed_grad * residual * inv_rms, axis=0, keepdims=True)
+    summed = lax.psum(jnp.concatenate([router_term, gain_term], axis=0), ("ctx", "exp"))
+    router_grad, gain_grad = summed[:EXPERTS].T, summed[EXPERTS]
     inner_mean = jnp.mean(residual * norm_gain * normed_grad, axis=1, keepdims=True)
     input_grad = (
         out_grad + norm_gain * inv_rms * normed_grad - residual * inv_rms**3 * inner_mean
@@ -218,38 +173,20 @@
     out_weight_grad = lax.psum_scatter(
         weight_part.astype(jnp.bfloat16), "ctx", scatter_dimension=1, tiled=True
     ).astype(jnp.float32)
-    attention_grad = attn_part.astype(jnp.bfloat16).reshape(tok_ctx, local_heads, HEAD_WIDTH)
-    delta_rows = jnp.sum(attention_grad.astype(jnp.float32) * attention.astype(jnp.float32), axis=2)
-
-    def release(query_acc, kv_block, anchor):
-        scores = block_scores(kv_block, anchor)
-        attn_probs = jnp.exp(scores - log_total[:, :, None])
-        prob_part = jnp.einsum(
-            "qhd,kd->qhk",
-            attention_grad,
-            kv_block[:, HEAD_WIDTH:],
-            preferred_element_type=jnp.float32,
+    attention_grad = attn_part.astype(jnp.bfloat16)
+    query_grads = []
+    for head in range(local_heads):
+        grad_head = columns(attention_grad, head)
+        delta = jnp.sum(
+            grad_head.astype(jnp.float32) * attention_heads[head].astype(jnp.float32),
+            axis=1,
+            keepdims=True,
         )
-        score_grad = (attn_probs * (prob_part - delta_rows[:, :, None])).astype(jnp.bfloat16)
-        return query_acc + jnp.einsum(
-            "qhk,kd->qhd", score_grad, kv_block[:, :HEAD_WIDTH], preferred_element_type=jnp.float32
-        )
-
-    query_acc = release(
-        jnp.zeros((tok_ctx, local_heads, HEAD_WIDTH), jnp.float32), own_block, ctx_index
-    )
-
-    def back_step(hop_count, query_sum):
-        anchor = ctx_index - hop_count
-        kv_block = lax.dynamic_index_in_dim(stored, jnp.maximum(anchor, 0), 0, keepdims=False)
-        return lax.cond(
-            hop_count <= ctx_index, lambda: release(query_sum, kv_block, anchor), lambda: query_sum
-        )
-
-    query_acc = lax.fori_loop(1, ctx_count, back_step, query_acc)
-    query_grad = (
-        (score_scale * query_acc).astype(jnp.bfloat16).reshape(tok_ctx, local_heads * HEAD_WIDTH)
-    )
+        attn_probs = jnp.exp(head_scores(head) - log_totals[head])
+        score_grad = (attn_probs * (dot_t(grad_head, values) - delta)).astype(jnp.bfloat16)
+        query_acc = jnp.dot(score_grad, keys, preferred_element_type=jnp.float32)
+        query_grads.append((score_scale * query_acc).astype(jnp.bfloat16))
+    query_grad = jnp.concatenate(query_grads, axis=1)
     return (
         layer_out,
         input_grad,

time: 625 us -> 586 us (0.938)
  blocking collectives: 41.4 us -> 11.5 us
  starting transfers between devices: 32.6 us -> 18.4 us
  matrix products: 62.4 us -> 69.7 us
    psum x1, waiting for transfers between devices: 6.25 us -> 177 us  [per_device(): lax.psum(jnp.concatenate([router_term, gain_term], axis=0), ('ctx', 'exp'))]
    reduce_scatter x1, waiting for transfers between devices: 121 us -> 17.7 us  [per_device(): lax.psum_scatter(gate_up_term.astype(jnp.bfloat16), 'ctx', scatter_dimens...]
    psum x1 -> x0, blocking collectives: 41.4 us -> none  [per_device(): router_grad, gain_grad = lax.psum((router_term, gain_term), ('ctx', 'exp'))]
    reduce_scatter x1, waiting for transfers between devices: 41 us -> 0.01 us  [per_device(): lax.psum_scatter(down_term.astype(jnp.bfloat16), 'ctx', scatter_dimension...]
    ppermute x3 -> x0, starting transfers between devices: 14.6 us -> none  [from_behind(): return lax.ppermute(shard, axis, pairs)]
    all_gather x0 -> x1, blocking collectives: none -> 11.5 us  [per_device(): all_kv = lax.all_gather(own_block, 'ctx', axis=0, tiled=True)]
    ppermute x3 -> x0, waiting for transfers between devices: 8.65 us -> none  [from_behind(): return lax.ppermute(shard, axis, pairs)]
    dot_general x4 -> x13, matrix products: 6.05 us -> 14.4 us  [the longest x4 8.43 us: per_device(): query_acc = jnp.dot(score_grad, keys, preferred_element_type=jnp.float32)]
  transfers between devices with their start and end apart: 15 -> 12, of which waited for: 13 -> 9; matrix products, arithmetic and copies ran while one was open for 11% -> 15% of each run, Pallas kernels for 0% -> 0%
where the time goes in v2:
time: 586 us; the launch traced here: 584 us
  waiting for transfers between devices  411 us (70%)
  matrix products  69.7 us (12%)
  local copies, waits for them, and re-layouts  34.3 us (6%)
  other arithmetic  23.5 us (4%)
  starting transfers between devices  18.4 us (3%)
  between operations  16.2 us (3%)
  blocking collectives  11.5 us (2%)
    psum x1, waiting for transfers between devices, per_device(): lax.psum(jnp.concatenate([router_term, gain_term], axis=0), ('ctx', 'exp'))  177 us
    all_gather x1, waiting for transfers between devices, per_device(): lax.all_gather(expert_down, 'ctx', axis=1, tiled=True)  60.7 us
    all_to_all x1, waiting for transfers between devices, per_device(): lax.all_to_all(grad_outgoing, 'exp', split_axis=0, concat_axis=1, tiled=T...  35.2 us
    all_to_all x1, waiting for transfers between devices, per_device(): lax.all_to_all(outgoing, 'exp', split_axis=0, concat_axis=1, tiled=True)  33.9 us
    reduce_scatter x1, waiting for transfers between devices, per_device(): lax.psum_scatter(jnp.dot(rows_here, out_weight, preferred_element_type=jn...  30.9 us
    all_to_all x1, waiting for transfers between devices, per_device(): lax.all_to_all(rows_back, 'exp', split_axis=1, concat_axis=0, tiled=True)  18.7 us
    all_to_all x1, waiting for transfers between devices, per_device(): lax.all_to_all(expert_out, 'exp', split_axis=1, concat_axis=0, tiled=True)  18.2 us
    all_gather x1, waiting for transfers between devices, per_device(): arriving = lax.all_gather(input_grad, 'exp', axis=0, tiled=True)  17.7 us
  transfers between devices with their start and end apart: 12, of which 9 were waited for; matrix products, arithmetic and copies ran while one was open for 15% of the time, Pallas kernels for 0%

profile of v2, /device:TPU:0, one launch (start us, length us, event | category | flops | bytes accessed | tf_op | source)
XLA Modules:
  0.0 584.4 jit_solution(3008243525728637320)
XLA Ops:
  9.2 11.5 %all_gather.12 = bf16[1024,256]{1,0:T(8,128)(2,1)S(1)} all-gather(bf16[256,256]{1,0:T(8,128)(2,1)S(1)} %constant_dynamic-slice_fusion), channel_id=1, replica_groups=mesh['ctx'=4,'exp'=8] {'ctx'}, dimensions={0}, use_global_device_ids=true | all-gather | bytes 655360 | tf_op jit(solution)/shard_map/all_gather | solution.py:38
  32.4 30.9 %reduce-scatter.5.cloned.1.call-done = bf16[32,2048]{1,0:T(8,128)(2,1)} async-done(((bf16[256,2048]{1,0:T(8,128)(2,1)}), bf16[32,2048]{1,0:T(8,128)(2,1)}) %reduce-scatter.5.cloned.1.call-update) | async-done | bytes 131088 | tf_op jit(solution)/shard_map/reduce_scatter | solution.py:64
  71.1 4.4 all-to-all-start.2
  78.1 35.2 %all-to-all-done.2 = bf16[16,18,2048]{2,1,0:T(8,128)(2,1)} async-done(((bf16[16,18,2048]{2,1,0:T(8,128)(2,1)}), bf16[16,18,2048]{2,1,0:T(8,128)(2,1)}, u32[]{:S(2)}, u32[]{:S(2)}) %all-to-all-start.2) | async-done | bytes 1179680 | tf_op jit(solution)/shard_map/all_to_all | solution.py:118
  113.3 4.5 all-to-all-start
  117.8 3.7 copy.93
  121.5 33.9 %all-to-all-done = bf16[16,18,2048]{2,1,0:T(8,128)(2,1)} async-done(((bf16[16,18,2048]{2,1,0:T(8,128)(2,1)}), bf16[16,18,2048]{2,1,0:T(8,128)(2,1)}, u32[]{:S(2)}, u32[]{:S(2)}) %all-to-all-start) | async-done | bytes 1179680 | tf_op jit(solution)/shard_map/all_to_all | solution.py:89
  158.1 8.1 %fusion.46 = f32[2,144,1536]{2,1,0:T(8,128)} fusion(bf16[2,2048,1536]{2,1,0:T(8,128)(2,1)} %all-gather.4.cloned.1.call-done, bf16[2,144,2048]{2,0,1:T(2,128)(2,1)S(1)} %bitcast.59), kind=kOutput, calls=%fused_computation.76 | convolution fusion | flops 1811939328 | bytes 15532032 | tf_op jit(solution)/shard_map/erd,edf->erf/dot_general | solution.py:94
  166.2 60.7 %all-gather.6.cloned.1.call-done = bf16[2,768,2048]{2,1,0:T(8,128)(2,1)} async-done(((bf16[2,192,2048]{2,1,0:T(8,128)(2,1)}), bf16[2,768,2048]{2,1,0:T(8,128)(2,1)}) %all-gather.6.cloned.1.call-update) | async-done | bytes 6291472 | tf_op jit(solution)/shard_map/all_gather | solution.py:92
  226.8 7.1 %multiply_convert_fusion.2 = (bf16[2,144,768]{2,1,0:T(8,128)(2,1)}, bf16[2,144,768]{2,1,0:T(8,128)(2,1)}, bf16[2,144,768]{2,1,0:T(8,128)(2,1)S(1)}) fusion(f32[2,144,1536]{2,1,0:T(8,128)} %fusion.46, bf16[2,768,2048]{2,1,0:T(8,128)(2,1)} %all-gather.6.cloned.1.call-done, bf16[2,144,2048]{2,0,1:T(2,128)(2,1)} %bitcast.61), kind=kOutput, calls=%fused_computation.88 | convolution fusion | flops 909508608 | bytes 10567680 | tf_op jit(solution)/shard_map/erd,efd->erf/dot_general | solution.py:120
  237.3 4.6 all-to-all-start.1
  241.9 9.1 %convolution_convert_fusion.4 = bf16[2,144,2048]{2,1,0:T(8,128)(2,1)S(1)} fusion(bf16[2,2048,1536]{2,1,0:T(8,128)(2,1)} %all-gather.4.cloned.1.call-done, bf16[2,144,768]{2,1,0:T(8,128)(2,1)} %get-tuple-element.57, bf16[2,144,768]{2,1,0:T(8,128)(2,1)} %get-tuple-element.56), kind=kOutput, calls=%fused_computation.5 | convolution fusion | flops 1814298624 | bytes 14647296 | tf_op jit(solution)/shard_map/erf,edf->erd/dot_general | solution.py:133
  253.2 18.2 %all-to-all-done.1 = bf16[2,144,2048]{2,0,1:T(2,128)(2,1)} async-done(((bf16[2,144,2048]{2,0,1:T(2,128)(2,1)}), bf16[2,144,2048]{2,0,1:T(2,128)(2,1)}, u32[]{:S(2)}, u32[]{:S(2)}) %all-to-all-start.1) | async-done | bytes 1179680 | tf_op jit(solution)/shard_map/all_to_all | solution.py:101
  271.4 4.3 all-to-all-start.3
  281.2 3.2 multiply_reduce_fusion
  286.3 18.7 %all-to-all-done.3 = bf16[2,144,2048]{2,0,1:T(2,128)(2,1)} async-done(((bf16[2,144,2048]{2,0,1:T(2,128)(2,1)}), bf16[2,144,2048]{2,0,1:T(2,128)(2,1)}, u32[]{:S(2)}, u32[]{:S(2)}) %all-to-all-start.3) | async-done | bytes 1179680 | tf_op jit(solution)/shard_map/all_to_all | solution.py:136
  317.4 17.7 %all-gather.8.cloned.1.call-done = bf16[256,2048]{1,0:T(8,128)(2,1)} async-done(((bf16[32,2048]{1,0:T(8,128)(2,1)}), bf16[256,2048]{1,0:T(8,128)(2,1)}) %all-gather.8.cloned.1.call-update) | async-done | bytes 1048592 | tf_op jit(solution)/shard_map/all_gather | solution.py:167
  335.1 3.4 convolution_convert_fusion.2
  338.6 6.0 %convolution_convert_fusion.1 = bf16[2,768,2048]{2,1,0:T(8,128)(2,1)} fusion(bf16[2,144,768]{2,1,0:T(8,128)(2,1)} %copy-done.2, bf16[2,144,2048]{2,0,1:T(2,128)(2,1)} %bitcast.62), kind=kOutput, calls=%fused_computation.1 | convolution fusion | flops 909115392 | bytes 7913472 | tf_op jit(solution)/shard_map/erf,erd->efd/dot_general | solution.py:127
  345.0 7.8 %convolution_convert_fusion = bf16[2,2048,1536]{2,1,0:T(8,128)(2,1)} fusion(bf16[2,144,2048]{2,0,1:T(2,128)(2,1)S(1)} %bitcast.60, bf16[2,144,768]{2,1,0:T(8,128)(2,1)} %get-tuple-element.57, bf16[2,144,768]{2,1,0:T(8,128)(2,1)} %get-tuple-element.56), kind=kOutput, calls=%fused_computation | convolution fusion | flops 1820000256 | bytes 14647296 | tf_op jit(solution)/shard_map/erd,erf->edf/dot_general | solution.py:130
  355.8 176.7 %all-reduce.2.cloned.1.call-done = f32[17,2048]{1,0:T(8,128)} async-done(((f32[17,2048]{1,0:T(8,128)}), f32[17,2048]{1,0:T(8,128)}) %all-reduce.2.cloned.1.call-update) | async-done | bytes 139280 | tf_op jit(solution)/shard_map/psum | solution.py:161
  550.2 3.7 convert_element_type.199
  553.9 17.7 %reduce-scatter.9.cloned.1.call-done = bf16[2,512,1536]{2,1,0:T(8,128)(2,1)} async-done(((bf16[2,2048,1536]{2,1,0:T(8,128)(2,1)}), bf16[2,512,1536]{2,1,0:T(8,128)(2,1)}) %reduce-scatter.9.cloned.1.call-update) | async-done | bytes 3145744 | tf_op jit(solution)/shard_map/reduce_scatter | solution.py:138
  571.6 5.5 convert_element_type.197
  (208 shorter events, 71.7 us)
Async XLA Ops:
  8.0 20.5 %copy-start = (bf16[512,2048]{1,0:T(8,128)(2,1)S(1)}, bf16[512,2048]{1,0:T(8,128)(2,1)}, u32[]{:S(2)}) copy-start(bf16[512,2048]{1,0:T(8,128)(2,1)} %param.13) | copy-start | bytes 6291460
  8.0 13.9 %copy-start.57 = (bf16[256,512]{1,0:T(8,128)(2,1)S(1)}, bf16[256,512]{1,0:T(8,128)(2,1)}, u32[]{:S(2)}) copy-start(bf16[256,512]{1,0:T(8,128)(2,1)} %param.11) | copy-start | bytes 786436
  8.0 55.2 %reduce-scatter.5.cloned.1.call-start = ((), (), s32[]{:S(2)}) async-start(), calls=%async_computation.8 | async-start | bytes 1179648 | tf_op jit(solution)/shard_map/reduce_scatter | solution.py:64
  30.2 127.8 %all-gather.4.cloned.1.call-start = ((), (), s32[]{:S(2)}) async-start(), calls=%async_computation.9 | async-start | bytes 15728640 | tf_op jit(solution)/shard_map/all_gather | solution.py:91
  30.8 32.5 %copy-start.3 = (bf16[32,2048]{1,0:T(8,128)(2,1)S(1)}, bf16[32,2048]{1,0:T(8,128)(2,1)}, u32[]{:S(2)}) copy-start(bf16[32,2048]{1,0:T(8,128)(2,1)} %param.10) | copy-start | bytes 393220
  30.8 34.1 %copy-start.29 = (f32[2048]{0:T(1024)S(1)}, f32[2048]{0:T(1024)}, u32[]{:S(2)}) copy-start(f32[2048]{0:T(1024)} %param.14) | copy-start | bytes 24580
  30.8 35.1 %copy-start.26 = (bf16[2048,16]{0,1:T(8,128)(2,1)S(1)}, bf16[2048,16]{0,1:T(8,128)(2,1)}, u32[]{:S(2)}) copy-start(bf16[2048,16]{0,1:T(8,128)(2,1)} %param.15) | copy-start | bytes 196612
  30.9 195.9 %all-gather.6.cloned.1.call-start = ((), (), s32[]{:S(2)}) async-start(), calls=%async_computation.10 | async-start | bytes 7864320 | tf_op jit(solution)/shard_map/all_gather | solution.py:92
  31.5 35.8 %copy-start.12 = (f32[32,2048]{1,0:T(8,128)}, f32[32,2048]{1,0:T(8,128)S(1)}, u32[]{:S(2)}) copy-start(f32[32,2048]{1,0:T(8,128)S(1)} %convert_element_type.172) | copy-start | bytes 786436
  65.9 9.7 %copy-start.5 = (bf16[32,2048]{1,0:T(8,128)(2,1)}, bf16[32,2048]{1,0:T(8,128)(2,1)S(1)}, u32[]{:S(2)}) copy-start(bf16[32,2048]{1,0:T(8,128)(2,1)S(1)} %multiply_convert_fusion.4) | copy-start | bytes 393220
  71.1 4.4 copy-start.33
  71.1 42.2 %all-to-all-start.2 = ((bf16[16,18,2048]{2,1,0:T(8,128)(2,1)}), bf16[16,18,2048]{2,1,0:T(8,128)(2,1)}, u32[]{:S(2)}, u32[]{:S(2)}) async-start(bf16[16,18,2048]{2,1,0:T(8,128)(2,1)} %reshape.197), calls=%async_computation.3 | async-start | bytes 3145728 | tf_op jit(solution)/shard_map/all_to_all | solution.py:118
  113.3 42.1 %all-to-all-start = ((bf16[16,18,2048]{2,1,0:T(8,128)(2,1)}), bf16[16,18,2048]{2,1,0:T(8,128)(2,1)}, u32[]{:S(2)}, u32[]{:S(2)}) async-start(bf16[16,18,2048]{2,1,0:T(8,128)(2,1)} %reshape.195), calls=%async_computation.1 | async-start | bytes 3145728 | tf_op jit(solution)/shard_map/all_to_all | solution.py:89
  226.8 7.1 %copy-start.1 = (bf16[2,768,2048]{2,1,0:T(8,128)(2,1)S(1)}, bf16[2,768,2048]{2,1,0:T(8,128)(2,1)}, u32[]{:S(2)}) copy-start(bf16[2,768,2048]{2,1,0:T(8,128)(2,1)} %all-gather.6.cloned.1.call-done) | copy-start | bytes 18874372
  237.3 34.1 %all-to-all-start.1 = ((bf16[2,144,2048]{2,0,1:T(2,128)(2,1)}), bf16[2,144,2048]{2,0,1:T(2,128)(2,1)}, u32[]{:S(2)}, u32[]{:S(2)}) async-start(bf16[2,144,2048]{2,0,1:T(2,128)(2,1)} %copy.89), calls=%async_computation.2 | async-start | bytes 2359296 | tf_op jit(solution)/shard_map/all_to_all | solution.py:101
  253.2 22.5 %copy-start.34 = (s32[32,8]{0,1:T(8,128)S(1)}, s32[32,8]{0,1:T(8,128)}, u32[]{:S(2)}) copy-start(s32[32,8]{0,1:T(8,128)} %multiply_add_fusion) | copy-start | bytes 3076
  271.4 33.6 %all-to-all-start.3 = ((bf16[2,144,2048]{2,0,1:T(2,128)(2,1)}), bf16[2,144,2048]{2,0,1:T(2,128)(2,1)}, u32[]{:S(2)}, u32[]{:S(2)}) async-start(bf16[2,144,2048]{2,0,1:T(2,128)(2,1)} %copy.95), calls=%async_computation.4 | async-start | bytes 2359296 | tf_op jit(solution)/shard_map/all_to_all | solution.py:136
  275.6 59.5 %all-gather.8.cloned.1.call-start = ((), (), s32[]{:S(2)}) async-start(), calls=%async_computation.11 | async-start | bytes 1179648 | tf_op jit(solution)/shard_map/all_gather | solution.py:167
  314.8 217.7 %all-reduce.2.cloned.1.call-start = ((), (), s32[]{:S(2)}) async-start(), calls=%async_computation.15 | async-start | bytes 393216 | tf_op jit(solution)/shard_map/psum | solution.py:161
  317.4 230.7 %reduce-scatter.7.cloned.1.call-start = ((), (), s32[]{:S(2)}) async-start(), calls=%async_computation.12 | async-start | bytes 2621440 | tf_op jit(solution)/shard_map/reduce_scatter | solution.py:173
  338.5 211.7 %reduce-scatter.11.cloned.1.call-start = ((), (), s32[]{:S(2)}) async-start(), calls=%async_computation.14 | async-start | bytes 7864320 | tf_op jit(solution)/shard_map/reduce_scatter | solution.py:141
  344.7 227.0 %reduce-scatter.9.cloned.1.call-start = ((), (), s32[]{:S(2)}) async-start(), calls=%async_computation.13 | async-start | bytes 15728640 | tf_op jit(solution)/shard_map/reduce_scatter | solution.py:138
  539.4 4.7 copy-start.7
  539.4 4.7 copy-start.55
  (46 other events, 91.0 us)
Sparse Core Ops, SparseCore 0:
  30.3 32.8 reduce-scatter.4
  314.9 20.1 all-gather.7
  341.2 191.2 all-reduce.1
Sparse Core Ops, SparseCore 1:
  32.6 122.5 all-gather.3
  156.9 69.9 all-gather.5
  338.6 34.9 reduce-scatter.6
  377.2 70.1 reduce-scatter.10
  450.5 121.1 reduce-scatter.8
